TPU v7x, 32 devices: a whole 2x2x4 slice. The times are simulated.
32 devices in a mesh: grp: 2 (over core), seq: 4 (over y, x), row: 4 (over z).
Axes of the slice: x: 2, y: 2, z: 4, core: 2. Of those that a mesh axis runs over, the one named last changes fastest.
Arguments:
- tokens: bfloat16 [512, 70, 1150], P(('grp', 'seq')), may hold values from -6 to 6
- in_mask: int32 [512, 1150], P(('grp', 'seq')), may hold values 0 or 1
- out_mask: int32 [512, 400], P(('grp', 'seq')), may hold values 0 or 1
- lengths: int32 [512], P(('grp', 'seq')), may hold values from 35 to 70, as said below
- groups: int32 [512], P(('grp', 'seq')), may hold values from 0 to 1, as said below
- input_gate_weight: bfloat16 [1600, 1150], P('row'), may hold values from -0.1875 to 0.1875
- w_recur: bfloat16 [1600, 400], P('row'), may hold values from -0.3125 to 0.3125
- weight_mask: int32 [1600, 400], P('row'), may hold values 0 or 1
- bias: float32 [1600], P('row'), may hold values from -3 to 3
- cotangent: bfloat16 [512, 70, 400], P(('grp', 'seq')), may hold values from -6 to 6
Outputs:
- input_grad: float32 [512, 70, 1150], P(('grp', 'seq', 'row'))
- grad_input_weight: float32 [2, 1600, 1150], P('grp', 'row')
- grad_recur_weight: float32 [2, 1600, 400], P('grp', 'row')
- grad_bias: float32 [2, 1600], P('grp', 'row')
- gram: float32 [2, 2], replicated
Inputs may be any that keep to these rules, and one draw needn't show every extreme that they name: `lengths`: each sequence has the full length or fewer steps; some sequence of the batch has exactly 70 steps and some exactly 35. Both groups have sequences.
All inputs are finite; a program needn't handle non-finite values. No bound on the sum of `in_mask` or of `out_mask` or of `weight_mask` on one device may be relied on, other than what follows from the above.
Results may differ from a plain program's by a relative error of at most 0.0063.
Values may be sent and summed in bfloat16 or wider, within the bound.
No kernel may reach another device: no remote copies, remote signals or barrier semaphores. Data moves between devices by JAX's collectives and lax.ppermute only.
A program may use at most 256 MiB of HBM per device.

v0:
```python
import jax
import jax.numpy as jnp
from jax import lax
from jax.sharding import PartitionSpec as P

ACTIVATION_COEF = 2.0
TAR_BETA = 1.0
KEEP_INPUT = 0.75
KEEP_OUTPUT = 0.6
KEEP_WEIGHT = 0.5


def swapped(block, axis, stride):
    count = lax.axis_size(axis)
    route = []
    for low in range(count):
        high = low | 1 << stride
        if high != low and high < count:
            route += [(low, high), (high, low)]
    return lax.ppermute(block, axis, route)


def gate_split(values, hidden):
    return (
        jax.nn.sigmoid(values[:, :hidden]),
        jax.nn.sigmoid(values[:, hidden : 2 * hidden]),
        jnp.tanh(values[:, 2 * hidden : 3 * hidden]),
        jax.nn.sigmoid(values[:, 3 * hidden :]),
    )


def local(
    tokens,
    in_mask,
    out_mask,
    lengths,
    groups,
    input_gate_weight,
    w_recur,
    weight_mask,
    bias,
    cotangent,
):
    seq_count, time_steps, width_in = tokens.shape
    hidden = cotangent.shape[2]
    row_count = input_gate_weight.shape[0]
    row_start = lax.axis_index("row") * row_count
    share = seq_count // lax.axis_size("row")
    share_start = lax.axis_index("row") * share
    group_hot = (groups[:, None] == jnp.arange(2)[None, :]).astype(jnp.float32)
    valid_mask = (jnp.arange(time_steps)[None, :] < lengths[:, None]).astype(jnp.float32)
    local_counts = jnp.sum(group_hot * jnp.sum(valid_mask, 1)[:, None], 0)
    counts = lax.psum(local_counts, ("grp", "seq"))
    group_ratio = jnp.sum(counts) / counts
    seq_ratio = jnp.sum(group_hot * group_ratio[None, :], 1)
    in_scale = in_mask.astype(jnp.float32) / KEEP_INPUT
    dropped_weight = (tokens.astype(jnp.float32) * in_scale[:, None, :]).astype(jnp.bfloat16)
    w_scale = weight_mask.astype(jnp.float32) / KEEP_WEIGHT
    w_eff = (w_recur.astype(jnp.float32) * w_scale).astype(jnp.bfloat16)
    projected = (
        jnp.einsum(
            "thw,aw->hta", dropped_weight, input_gate_weight, preferred_element_type=jnp.float32
        )
        + bias[None, None, :]
    )
    zero_state = jnp.zeros((seq_count, hidden), jnp.float32)

    def full_gates(proj_step, hidden_low):
        partial_gates = proj_step + jnp.einsum(
            "sh,rh->sr", hidden_low, w_eff, preferred_element_type=jnp.float32
        )
        return lax.all_gather(partial_gates, "row", axis=1, tiled=True)

    def recur_back(pre_grad):
        own_rows = lax.dynamic_slice_in_dim(pre_grad, row_start, row_count, 1)
        partial_back = jnp.dot(own_rows, w_eff, preferred_element_type=jnp.float32)
        return lax.psum(partial_back, "row")

    def forward_step(carry, proj_step):
        cell_state, hidden_low = carry
        pre_act = full_gates(proj_step, hidden_low)
        gate_input_part, gate_forget, gate_cell, gate_output_part = gate_split(pre_act, hidden)
        new_cell = gate_forget * cell_state + gate_input_part * gate_cell
        new_hidden = gate_output_part * jnp.tanh(new_cell)
        stored = jnp.concatenate([gate_input_part, gate_forget, gate_cell, gate_output_part], 1)
        return ((new_cell, new_hidden.astype(jnp.bfloat16)), (stored, new_cell, new_hidden))

    start_state = (zero_state, zero_state.astype(jnp.bfloat16))
    _, (activations, cell_seq, hidden_seq) = lax.scan(forward_step, start_state, projected)
    out_scale = out_mask.astype(jnp.float32) / KEEP_OUTPUT
    cot_time = jnp.swapaxes(cotangent, 0, 1).astype(jnp.float32)
    valid_time = valid_mask.T
    outputs = hidden_seq * out_scale[None]
    out_grad = valid_time[:, :, None] * (
        cot_time + 2.0 * ACTIVATION_COEF * seq_ratio[None, :, None] * outputs
    )
    zero_row = jnp.zeros((1, seq_count, hidden), jnp.float32)
    hidden_prev = jnp.concatenate([zero_row, hidden_seq[:-1]], 0)
    later = (jnp.arange(time_steps) >= 1).astype(jnp.float32)
    smooth_weight = 2.0 * TAR_BETA * seq_ratio[None, :] * valid_time * later[:, None]
    smooth_term = smooth_weight[:, :, None] * (hidden_seq - hidden_prev)
    direct_grad = (
        out_grad * out_scale[None] + smooth_term - jnp.concatenate([smooth_term[1:], zero_row], 0)
    )
    cell_prev = jnp.concatenate([zero_row, cell_seq[:-1]], 0)

    def backward_step(carry, inputs_now):
        cell_grad, recur_grad = carry
        direct_now, stored, cell_state, cell_before = inputs_now
        gate_input_part = stored[:, :hidden]
        gate_forget = stored[:, hidden : 2 * hidden]
        gate_cell = stored[:, 2 * hidden : 3 * hidden]
        gate_output_part = stored[:, 3 * hidden :]
        hidden_grad = direct_now + recur_grad
        tanh_cell = jnp.tanh(cell_state)
        total_cell = cell_grad + hidden_grad * gate_output_part * (1.0 - tanh_cell * tanh_cell)
        pre_grad = jnp.concatenate(
            [
                total_cell * gate_cell * gate_input_part * (1.0 - gate_input_part),
                total_cell * cell_before * gate_forget * (1.0 - gate_forget),
                total_cell * gate_input_part * (1.0 - gate_cell * gate_cell),
                hidden_grad * tanh_cell * gate_output_part * (1.0 - gate_output_part),
            ],
            1,
        ).astype(jnp.bfloat16)
        own_rows = lax.dynamic_slice_in_dim(pre_grad, row_start, row_count, 1)
        share_rows = lax.dynamic_slice_in_dim(pre_grad, share_start, share, 0)
        new_carry = (total_cell * gate_forget, recur_back(pre_grad))
        return (new_carry, (own_rows, share_rows[:, :0]))

    _, (pre_grads, share_grads) = lax.scan(
        backward_step,
        (zero_state, zero_state),
        (direct_grad, activations, cell_seq, cell_prev),
        reverse=True,
    )
    grad_seq = jnp.swapaxes(pre_grads, 0, 1)
    prev_low = jnp.swapaxes(hidden_prev, 0, 1).astype(jnp.bfloat16)
    grads_in = []
    grads_rec = []
    bias_gradient_rows = []
    for group_index in range(2):
        selector = (groups == group_index).astype(jnp.bfloat16)
        masked = grad_seq * selector[:, None, None]
        grads_in.append(
            jnp.einsum("slr,slk->rk", masked, dropped_weight, preferred_element_type=jnp.float32)
        )
        grads_rec.append(
            jnp.einsum("slr,slh->rh", masked, prev_low, preferred_element_type=jnp.float32)
            * w_scale
        )
        bias_gradient_rows.append(jnp.sum(masked.astype(jnp.float32), (0, 1)))
    stacked = (jnp.stack(grads_in), jnp.stack(grads_rec), jnp.stack(bias_gradient_rows))
    own_scale = lax.dynamic_slice_in_dim(in_scale, share_start, share, 0)
    input_sum = lax.psum_scatter(
        jnp.einsum("slr,rk->slk", grad_seq, input_gate_weight, preferred_element_type=jnp.float32),
        "row",
        scatter_dimension=0,
        tiled=True,
    )
    input_grad = input_sum * own_scale[:, None, :]
    own_grads = (
        lax.psum_scatter(stacked[0], "grp", scatter_dimension=0, tiled=True),
        lax.psum_scatter(stacked[1], "grp", scatter_dimension=0, tiled=True),
        lax.psum_scatter(stacked[2], "grp", scatter_dimension=0, tiled=True),
    )
    own_grads = lax.psum((own_grads[0], own_grads[1], own_grads[2]), "seq")
    flat_own = jnp.concatenate([member.reshape(-1) for member in own_grads])
    flat_peer = swapped(flat_own.astype(jnp.bfloat16), "grp", 0).astype(flat_own.dtype)
    self_dot = jnp.sum(flat_own * flat_own)
    cross_dot = jnp.sum(flat_own * flat_peer)
    mine_hot = (jnp.arange(2) == lax.axis_index("grp")).astype(jnp.float32)
    local_gram = (
        mine_hot[:, None] * mine_hot[None, :] * self_dot
        + mine_hot[:, None] * (1.0 - mine_hot)[None, :] * cross_dot
    )
    gram = lax.psum(local_gram, ("grp", "row"))
    grad_in, grad_rec, grad_bias = own_grads
    return (input_grad, grad_in, grad_rec, grad_bias, gram)


def solution(mesh):
    return jax.shard_map(
        local,
        mesh=mesh,
        in_specs=(
            P(("grp", "seq"), None, None),
            P(("grp", "seq"), None),
            P(("grp", "seq"), None),
            P(("grp", "seq")),
            P(("grp", "seq")),
            P("row", None),
            P("row", None),
            P("row", None),
            P("row"),
            P(("grp", "seq"), None, None),
        ),
        out_specs=(
            P(("grp", "seq", "row"), None, None),
            P("grp", "row", None),
            P("grp", "row", None),
            P("grp", "row"),
            P(),
        ),
        check_vma=False,
    )
```

profile of v0, /device:TPU:0, one launch (start us, length us, event | category | flops | bytes accessed | tf_op | source)
XLA Modules:
  0.0 4704.8 jit_solution(5779984104247842560)
XLA Ops:
  33.6 1463.2 %while.38 = (s32[]{:T(128)}, f32[64,400]{1,0:T(8,128)S(1)}, bf16[64,400]{1,0:T(8,128)(2,1)S(1)}, f32[70,64,1600]{2,1,0:T(8,128)}, f32[70,64,400]{2,1,0:T(8,128)}...) while((s32[]{:T(128)}, f32[64,400]{1,0:T(8,128)S(1)}, ...), condition=%wide.region_6.7_spmd.clone, body=%wide.region_5.6_spmd.clone.sunk | while | flops 21171204 | bytes 6539380 | solution.py:89
  1560.0 2709.5 %while.39 = (s32[]{:T(128)}, f32[64,400]{1,0:T(8,128)S(1)}, f32[64,400]{1,0:T(8,128)}, bf16[70,64,400]{2,1,0:T(8,128)(2,1)}, f32[70,64,400]{2,1,0:T(8,128)}, /*i...) while((s32[]{:T(128)}, f32[64,400]{1,0:T(8,128)S(1)}, ...), condition=%wide.region_9.10_spmd.clone, body=%wide.region_7.9_spmd.clone.sunk | while | flops 21222404 | bytes 4233935 | solution.py:131
  1565.1 36.2 all-reduce.10.cloned.1.call-done
  1606.4 33.6 all-reduce.10.cloned.1.call-done
  1645.0 33.6 all-reduce.10.cloned.1.call-done
  1683.7 33.6 all-reduce.10.cloned.1.call-done
  1722.4 33.5 all-reduce.10.cloned.1.call-done
  1761.1 33.6 all-reduce.10.cloned.1.call-done
  1799.7 33.6 all-reduce.10.cloned.1.call-done
  1838.4 33.6 all-reduce.10.cloned.1.call-done
  1877.1 33.5 all-reduce.10.cloned.1.call-done
  1915.7 33.6 all-reduce.10.cloned.1.call-done
  1954.4 33.6 all-reduce.10.cloned.1.call-done
  1993.1 33.6 all-reduce.10.cloned.1.call-done
  2031.8 33.5 all-reduce.10.cloned.1.call-done
  2070.4 33.6 all-reduce.10.cloned.1.call-done
  2109.1 33.6 all-reduce.10.cloned.1.call-done
  2147.8 33.6 all-reduce.10.cloned.1.call-done
  2186.4 33.5 all-reduce.10.cloned.1.call-done
  2225.1 33.6 all-reduce.10.cloned.1.call-done
  2263.8 33.6 all-reduce.10.cloned.1.call-done
  2302.4 33.6 all-reduce.10.cloned.1.call-done
  2341.1 33.5 all-reduce.10.cloned.1.call-done
  2379.8 33.6 all-reduce.10.cloned.1.call-done
  2418.4 33.6 all-reduce.10.cloned.1.call-done
  2457.1 33.6 all-reduce.10.cloned.1.call-done
  2495.8 33.5 all-reduce.10.cloned.1.call-done
  2534.4 33.6 all-reduce.10.cloned.1.call-done
  2573.1 33.6 all-reduce.10.cloned.1.call-done
  2611.8 33.6 all-reduce.10.cloned.1.call-done
  2689.1 33.6 all-reduce.10.cloned.1.call-done
  2727.8 33.6 all-reduce.10.cloned.1.call-done
  2766.5 33.6 all-reduce.10.cloned.1.call-done
  2805.1 33.5 all-reduce.10.cloned.1.call-done
  2843.8 33.6 all-reduce.10.cloned.1.call-done
  2882.5 33.6 all-reduce.10.cloned.1.call-done
  2921.2 33.6 all-reduce.10.cloned.1.call-done
  2998.5 33.6 all-reduce.10.cloned.1.call-done
  3037.2 33.6 all-reduce.10.cloned.1.call-done
  3075.8 33.6 all-reduce.10.cloned.1.call-done
  3153.2 33.6 all-reduce.10.cloned.1.call-done
  3191.8 33.6 all-reduce.10.cloned.1.call-done
  3230.5 33.6 all-reduce.10.cloned.1.call-done
  3307.8 33.6 all-reduce.10.cloned.1.call-done
  3346.5 33.6 all-reduce.10.cloned.1.call-done
  3385.2 33.6 all-reduce.10.cloned.1.call-done
  3462.5 33.6 all-reduce.10.cloned.1.call-done
  3501.2 33.6 all-reduce.10.cloned.1.call-done
  3539.9 33.6 all-reduce.10.cloned.1.call-done
  3617.2 33.6 all-reduce.10.cloned.1.call-done
  3655.9 33.6 all-reduce.10.cloned.1.call-done
  3694.5 33.6 all-reduce.10.cloned.1.call-done
  3771.9 33.6 all-reduce.10.cloned.1.call-done
  3810.5 33.6 all-reduce.10.cloned.1.call-done
  3849.2 33.6 all-reduce.10.cloned.1.call-done
  3926.5 33.6 all-reduce.10.cloned.1.call-done
  3965.2 33.6 all-reduce.10.cloned.1.call-done
  4003.9 33.6 all-reduce.10.cloned.1.call-done
  4081.2 33.6 all-reduce.10.cloned.1.call-done
  4119.9 33.6 all-reduce.10.cloned.1.call-done
  4158.6 33.6 all-reduce.10.cloned.1.call-done
  4235.9 33.6 all-reduce.10.cloned.1.call-done
  4354.7 47.3 %all-reduce.8.cloned.1.call-done = (f32[1,400,1150]{2,1,0:T(8,128)}, f32[1,400,400]{2,1,0:T(8,128)}) async-done(((f32[1,400,1150]{2,1,0:T(8,128)}, f32[1,400,400]{2,1,0:T(8,128)}), (f32[1,400,1150]{2,1,0:T(8,128)}, f32[1,400,400]{2,1,0:T(8,128)})) %all-reduce.8.cloned.1.call-update) | async-done | bytes 2480016 | tf_op jit(solution)/shard_map/psum | solution.py:167
  4456.7 232.0 %reduce-scatter.4.cloned.1.call-done = f32[16,70,1150]{2,1,0:T(8,128)} async-done(((f32[64,70,1150]{2,1,0:T(8,128)}), f32[16,70,1150]{2,1,0:T(8,128)}) %reduce-scatter.4.cloned.1.call-update) | async-done | bytes 5152016 | tf_op jit(solution)/shard_map/reduce_scatter | solution.py:155
  (1365 shorter events, 2387.6 us)
Async XLA Ops:
  1560.0 41.3 all-reduce.10.cloned.1.call-start
  1601.3 38.7 all-reduce.10.cloned.1.call-start
  1639.9 38.7 all-reduce.10.cloned.1.call-start
  1678.6 38.7 all-reduce.10.cloned.1.call-start
  1717.3 38.6 all-reduce.10.cloned.1.call-start
  1755.9 38.7 all-reduce.10.cloned.1.call-start
  1794.6 38.7 all-reduce.10.cloned.1.call-start
  1833.3 38.7 all-reduce.10.cloned.1.call-start
  1872.0 38.6 all-reduce.10.cloned.1.call-start
  1910.6 38.7 all-reduce.10.cloned.1.call-start
  1949.3 38.7 all-reduce.10.cloned.1.call-start
  1988.0 38.7 all-reduce.10.cloned.1.call-start
  2026.7 38.6 all-reduce.10.cloned.1.call-start
  2065.3 38.7 all-reduce.10.cloned.1.call-start
  2104.0 38.7 all-reduce.10.cloned.1.call-start
  2142.7 38.7 all-reduce.10.cloned.1.call-start
  2181.3 38.6 all-reduce.10.cloned.1.call-start
  2220.0 38.7 all-reduce.10.cloned.1.call-start
  2258.7 38.7 all-reduce.10.cloned.1.call-start
  2297.3 38.7 all-reduce.10.cloned.1.call-start
  2336.0 38.6 all-reduce.10.cloned.1.call-start
  2374.7 38.7 all-reduce.10.cloned.1.call-start
  2413.3 38.7 all-reduce.10.cloned.1.call-start
  2452.0 38.7 all-reduce.10.cloned.1.call-start
  2490.7 38.6 all-reduce.10.cloned.1.call-start
  2529.3 38.7 all-reduce.10.cloned.1.call-start
  2568.0 38.7 all-reduce.10.cloned.1.call-start
  2606.7 38.7 all-reduce.10.cloned.1.call-start
  2684.0 38.7 all-reduce.10.cloned.1.call-start
  2722.7 38.7 all-reduce.10.cloned.1.call-start
  2761.4 38.7 all-reduce.10.cloned.1.call-start
  2838.7 38.7 all-reduce.10.cloned.1.call-start
  2877.4 38.7 all-reduce.10.cloned.1.call-start
  2916.0 38.7 all-reduce.10.cloned.1.call-start
  2993.4 38.7 all-reduce.10.cloned.1.call-start
  3032.0 38.7 all-reduce.10.cloned.1.call-start
  3070.7 38.7 all-reduce.10.cloned.1.call-start
  3109.4 38.6 all-reduce.10.cloned.1.call-start
  3148.0 38.7 all-reduce.10.cloned.1.call-start
  3186.7 38.7 all-reduce.10.cloned.1.call-start
  3225.4 38.7 all-reduce.10.cloned.1.call-start
  3302.7 38.7 all-reduce.10.cloned.1.call-start
  3341.4 38.7 all-reduce.10.cloned.1.call-start
  3380.1 38.7 all-reduce.10.cloned.1.call-start
  3457.4 38.7 all-reduce.10.cloned.1.call-start
  3496.1 38.7 all-reduce.10.cloned.1.call-start
  3534.8 38.7 all-reduce.10.cloned.1.call-start
  3612.1 38.7 all-reduce.10.cloned.1.call-start
  3650.8 38.7 all-reduce.10.cloned.1.call-start
  3689.4 38.7 all-reduce.10.cloned.1.call-start
  3728.1 38.6 all-reduce.10.cloned.1.call-start
  3766.8 38.7 all-reduce.10.cloned.1.call-start
  3805.4 38.7 all-reduce.10.cloned.1.call-start
  3844.1 38.7 all-reduce.10.cloned.1.call-start
  3921.4 38.7 all-reduce.10.cloned.1.call-start
  3960.1 38.7 all-reduce.10.cloned.1.call-start
  3998.8 38.7 all-reduce.10.cloned.1.call-start
  4076.1 38.7 all-reduce.10.cloned.1.call-start
  4114.8 38.7 all-reduce.10.cloned.1.call-start
  4153.5 38.7 all-reduce.10.cloned.1.call-start
  4192.1 38.6 all-reduce.10.cloned.1.call-start
  4230.8 38.7 all-reduce.10.cloned.1.call-start
  4307.2 94.8 %all-reduce.8.cloned.1.call-start = ((), (), s32[]{:S(2)}) async-start(), calls=%async_computation.6 | async-start | bytes 5324800 | tf_op jit(solution)/shard_map/psum | solution.py:167
  4318.5 370.2 %reduce-scatter.4.cloned.1.call-start = ((), (), s32[]{:S(2)}) async-start(), calls=%async_computation.3 | async-start | bytes 26542080 | tf_op jit(solution)/shard_map/reduce_scatter | solution.py:155
  (24 other events, 2511.2 us)
Sparse Core Ops, SparseCore 0:
  1564.5 36.7 all-reduce.9
  1605.8 34.1 all-reduce.9
  1644.4 34.1 all-reduce.9
  1683.1 34.1 all-reduce.9
  1721.8 34.1 all-reduce.9
  1760.4 34.1 all-reduce.9
  1799.1 34.1 all-reduce.9
  1837.8 34.1 all-reduce.9
  1876.5 34.1 all-reduce.9
  1915.1 34.1 all-reduce.9
  1953.8 34.1 all-reduce.9
  1992.5 34.1 all-reduce.9
  2031.2 34.1 all-reduce.9
  2069.8 34.1 all-reduce.9
  2108.5 34.1 all-reduce.9
  2147.2 34.1 all-reduce.9
  2185.8 34.1 all-reduce.9
  2224.5 34.1 all-reduce.9
  2263.2 34.1 all-reduce.9
  2301.8 34.1 all-reduce.9
  2340.5 34.1 all-reduce.9
  2379.2 34.1 all-reduce.9
  2417.8 34.1 all-reduce.9
  2456.5 34.1 all-reduce.9
  2495.2 34.1 all-reduce.9
  2533.8 34.1 all-reduce.9
  2572.5 34.1 all-reduce.9
  2611.2 34.1 all-reduce.9
  2649.9 34.1 all-reduce.9
  2688.5 34.1 all-reduce.9
  2727.2 34.1 all-reduce.9
  2765.9 34.1 all-reduce.9
  2804.5 34.1 all-reduce.9
  2843.2 34.1 all-reduce.9
  2881.9 34.1 all-reduce.9
  2920.5 34.1 all-reduce.9
  2959.2 34.1 all-reduce.9
  2997.9 34.1 all-reduce.9
  3036.5 34.1 all-reduce.9
  3075.2 34.1 all-reduce.9
  3113.9 34.1 all-reduce.9
  3152.5 34.1 all-reduce.9
  3191.2 34.1 all-reduce.9
  3229.9 34.1 all-reduce.9
  3307.2 34.1 all-reduce.9
  3345.9 34.1 all-reduce.9
  3384.6 34.1 all-reduce.9
  3461.9 34.1 all-reduce.9
  3500.6 34.1 all-reduce.9
  3539.3 34.1 all-reduce.9
  3616.6 34.1 all-reduce.9
  3655.3 34.1 all-reduce.9
  3693.9 34.1 all-reduce.9
  3771.3 34.1 all-reduce.9
  3809.9 34.1 all-reduce.9
  3848.6 34.1 all-reduce.9
  3925.9 34.1 all-reduce.9
  3964.6 34.1 all-reduce.9
  4003.3 34.1 all-reduce.9
  4080.6 34.1 all-reduce.9
  4119.3 34.1 all-reduce.9
  4158.0 34.1 all-reduce.9
  4235.3 34.1 all-reduce.9
  4335.5 353.1 reduce-scatter.3
  (7 shorter events, 238.4 us)
Sparse Core Ops, SparseCore 1:
  4284.0 8.7 reduce-scatter.7
  4307.3 11.1 reduce-scatter.5
  4321.9 80.1 all-reduce.7
where the time goes:
time: 4720 us; the launch traced here: 4700 us
  waiting for transfers between devices  2650 us (56%)
  blocking collectives  1150 us (24%)
  local copies, waits for them, and re-layouts  459 us (10%)
  other arithmetic  285 us (6%)
  matrix products  144 us (3%)
    psum x70, waiting for transfers between devices, recur_back(): return lax.psum(partial_back, 'row')  2350 us
    all_gather x70, blocking collectives, full_gates(): return lax.all_gather(partial_gates, 'row', axis=1, tiled=True)  1100 us
    reduce_scatter x1, waiting for transfers between devices, local(): lax.psum_scatter(jnp.einsum('slr,rk->slk', grad_seq, input_gate_weight, p...  232 us
    another operation x142, other arithmetic  156 us
    dynamic_update_slice x140, local copies, waits for them, and re-layouts, local(): lax.scan(forward_step, start_state, projected)  102 us
  transfers between devices with their start and end apart: 75, of which 74 were waited for; matrix products, arithmetic and copies ran while one was open for 3% of the time, Pallas kernels for 0%

commit v1 on v0

v1 whole, which is shorter than its diff:
```python
import functools

import jax
import jax.numpy as jnp
from jax import lax
from jax.experimental import pallas as pl
from jax.experimental.pallas import tpu as pltpu
from jax.sharding import PartitionSpec as P

ACTIVATION_COEF = 2.0
TAR_BETA = 1.0
KEEP_INPUT = 0.75
KEEP_OUTPUT = 0.6
KEEP_WEIGHT = 0.5
LANES = 128
VMEM_LIMIT = 56 << 20
BF16 = jnp.bfloat16
F32 = jnp.float32


def ceil_to(value, step):
    return -(-value // step) * step


def flip(block, axis, bit):
    count = lax.axis_size(axis)
    return lax.ppermute(block, axis, [(at, at ^ bit) for at in range(count)])


def butterfly_sum(block, axes):
    for axis in axes:
        count = lax.axis_size(axis)
        if count & (count - 1):
            block = lax.psum(block, axis)
            continue
        bit = 1
        while bit < count:
            block = block + flip(block, axis, bit)
            bit *= 2
    return block


def spread(block, axis):
    count = lax.axis_size(axis)
    copies = jnp.broadcast_to(block[None], (count,) + block.shape)
    return lax.all_to_all(copies, axis, 0, 0, tiled=True)


def sigmoid(value):
    return 0.5 * jnp.tanh(0.5 * value) + 0.5


def forward_kernel(
    hid, drop_ref, win_ref, wrec_ref, act_ref, cell_ref, prev_ref, proj, cell_s, low_s
):
    steps, seqs, width = drop_ref.shape

    @pl.when(pl.program_id(0) == 0)
    def _():
        cell_s[...] = jnp.zeros_like(cell_s)
        low_s[...] = jnp.zeros_like(low_s)

    rows = drop_ref[...].reshape(steps * seqs, width)
    proj[...] = jnp.dot(rows, win_ref[...], preferred_element_type=F32)
    cell = cell_s[...]
    low = low_s[...]
    for k in range(steps):
        prev_ref[k] = low
        pre = proj[k * seqs : (k + 1) * seqs] + jnp.dot(
            low, wrec_ref[...], preferred_element_type=F32
        )
        gate_i = sigmoid(pre[:, :hid])
        gate_f = sigmoid(pre[:, hid : 2 * hid])
        gate_g = jnp.tanh(pre[:, 2 * hid : 3 * hid])
        gate_o = sigmoid(pre[:, 3 * hid :])
        cell = gate_f * cell + gate_i * gate_g
        low = (gate_o * jnp.tanh(cell)).astype(BF16)
        act_ref[k, :, :hid] = gate_i
        act_ref[k, :, hid : 2 * hid] = gate_f
        act_ref[k, :, 2 * hid : 3 * hid] = gate_g
        act_ref[k, :, 3 * hid :] = gate_o
        cell_ref[k] = cell
    cell_s[...] = cell
    low_s[...] = low


def backward_kernel(
    hid,
    act_ref,
    cell_ref,
    before_ref,
    out_before_ref,
    cot_ref,
    scale_ref,
    act_coef_ref,
    smooth_ref,
    length_ref,
    wrec_ref,
    grad_ref,
    cell_grad_s,
    recur_s,
    smooth_s,
):
    steps, seqs, _ = act_ref.shape
    place = pl.program_id(0)
    block = pl.num_programs(0) - 1 - place

    @pl.when(place == 0)
    def _():
        cell_grad_s[...] = jnp.zeros_like(cell_grad_s)
        recur_s[...] = jnp.zeros_like(recur_s)
        smooth_s[...] = jnp.zeros_like(smooth_s)

    inner = (block > 0).astype(F32)
    dcell = cell_grad_s[...]
    recur = recur_s[...]
    smooth_next = smooth_s[...]
    scale = scale_ref[...]
    length = length_ref[...]
    cell = cell_ref[steps - 1]
    tanh_cell = jnp.tanh(cell)
    gate_o = act_ref[steps - 1, :, 3 * hid :]
    hidden = gate_o * tanh_cell
    for k in range(steps - 1, -1, -1):
        if k > 0:
            cell_before = cell_ref[k - 1]
            out_before = act_ref[k - 1, :, 3 * hid :]
        else:
            cell_before = before_ref[0] * inner
            out_before = out_before_ref[0]
        tanh_before = jnp.tanh(cell_before)
        hidden_before = out_before * tanh_before
        gate_i = act_ref[k, :, :hid]
        gate_f = act_ref[k, :, hid : 2 * hid]
        gate_g = act_ref[k, :, 2 * hid : 3 * hid]
        valid = length > block * steps + k
        smooth = smooth_ref[...] * (hidden - hidden_before)
        if k == 0:
            smooth = smooth * inner
        smooth = jnp.where(valid, smooth, 0.0)
        cot = cot_ref[k].astype(F32)
        direct = jnp.where(valid, scale * cot + act_coef_ref[...] * hidden, 0.0)
        dhidden = direct + smooth - smooth_next + recur
        smooth_next = smooth
        dcell = dcell + dhidden * gate_o * (1.0 - tanh_cell * tanh_cell)
        grad_ref[k, :, :hid] = (dcell * gate_g * gate_i * (1.0 - gate_i)).astype(BF16)
        grad_ref[k, :, hid : 2 * hid] = (dcell * cell_before * gate_f * (1.0 - gate_f)).astype(BF16)
        grad_ref[k, :, 2 * hid : 3 * hid] = (dcell * gate_i * (1.0 - gate_g * gate_g)).astype(BF16)
        grad_ref[k, :, 3 * hid :] = (dhidden * tanh_cell * gate_o * (1.0 - gate_o)).astype(BF16)
        dcell = dcell * gate_f
        recur = jnp.dot(grad_ref[k], wrec_ref[...], preferred_element_type=F32)
        tanh_cell = tanh_before
        hidden = hidden_before
        gate_o = out_before
    cell_grad_s[...] = dcell
    recur_s[...] = recur
    smooth_s[...] = smooth_next


def weight_kernel(rows_ref, drop_ref, prev_ref, pick_ref, in_ref, rec_ref):
    steps, seqs, own = rows_ref.shape

    @pl.when(pl.program_id(0) == 0)
    def _():
        in_ref[...] = jnp.zeros_like(in_ref)
        rec_ref[...] = jnp.zeros_like(rec_ref)

    grads = rows_ref[...]
    first = (grads * pick_ref[...][None]).reshape(steps * seqs, own)
    second = grads.reshape(steps * seqs, own) - first
    drop = drop_ref[...].reshape(steps * seqs, drop_ref.shape[2])
    prev = prev_ref[...].reshape(steps * seqs, prev_ref.shape[2])
    over = (((0,), (0,)), ((), ()))
    for at, part in enumerate((first, second)):
        in_ref[at] += lax.dot_general(part, drop, over, preferred_element_type=F32)
        rec_ref[at] += lax.dot_general(part, prev, over, preferred_element_type=F32)


def params(count=1):
    return pltpu.CompilerParams(
        dimension_semantics=("arbitrary",) * count, vmem_limit_bytes=VMEM_LIMIT
    )


def block_steps(time_steps, most):
    return max(s for s in range(1, most + 1) if time_steps % s == 0)


def local(
    tokens,
    in_mask,
    out_mask,
    lengths,
    groups,
    input_gate_weight,
    w_recur,
    weight_mask,
    bias,
    cotangent,
):
    seq_count, time_steps, width_in = tokens.shape
    hidden = cotangent.shape[2]
    row_count = input_gate_weight.shape[0]
    row_at = lax.axis_index("row")
    grp_at = lax.axis_index("grp")
    seq_at = lax.axis_index("seq")
    rows_n, grp_n, seq_n = (lax.axis_size(a) for a in ("row", "grp", "seq"))
    gates = rows_n * row_count
    hid = ceil_to(hidden, LANES)
    wide = ceil_to(width_in + 2, LANES)
    share = seq_count // rows_n
    pieces = grp_n * seq_n

    w_scale = weight_mask.astype(F32) / KEEP_WEIGHT
    w_eff = (w_recur.astype(F32) * w_scale).astype(BF16)
    bias_high = bias.astype(BF16)
    bias_low = (bias - bias_high.astype(F32)).astype(BF16)
    own_weights = jnp.concatenate(
        [input_gate_weight, bias_high[:, None], bias_low[:, None], w_eff], 1
    )
    piece_rows = ceil_to(row_count, pieces) // pieces
    padded = jnp.pad(own_weights, ((0, pieces * piece_rows - row_count), (0, 0)))
    mine = lax.dynamic_slice_in_dim(padded, (grp_at * seq_n + seq_at) * piece_rows, piece_rows, 0)
    got = spread(mine, "row")
    got = spread(got, "seq")
    got = spread(got, "grp")
    got = got.reshape(grp_n * seq_n, rows_n, piece_rows, -1)
    whole = jnp.swapaxes(got, 0, 1).reshape(rows_n, pieces * piece_rows, -1)[:, :row_count]
    whole = whole.reshape(4, hidden, -1)
    whole = jnp.pad(whole, ((0, 0), (0, hid - hidden), (0, 0))).reshape(4 * hid, -1)
    w_in = whole[:, : width_in + 2]
    w_rec = jnp.pad(whole[:, width_in + 2 :], ((0, 0), (0, hid - hidden)))
    w_in_t = jnp.pad(w_in.T, ((0, wide - width_in - 2), (0, 0)))
    w_rec_t = w_rec.T

    in_scale = in_mask.astype(F32) / KEEP_INPUT
    tok_time = jnp.swapaxes(tokens, 0, 1)
    dropped = (tok_time.astype(F32) * in_scale[None]).astype(BF16)
    dropped = jnp.concatenate(
        [
            dropped,
            jnp.ones((time_steps, seq_count, 2), BF16),
            jnp.zeros((time_steps, seq_count, wide - width_in - 2), BF16),
        ],
        2,
    )
    cot_time = jnp.pad(jnp.swapaxes(cotangent, 0, 1), ((0, 0), (0, 0), (0, hid - hidden)))

    group_hot = (groups[:, None] == jnp.arange(2)[None, :]).astype(F32)
    valid_count = jnp.clip(lengths, 0, time_steps).astype(F32)
    local_counts = jnp.sum(group_hot * valid_count[:, None], 0)
    counts = butterfly_sum(local_counts, ("grp", "seq"))
    group_ratio = jnp.sum(counts) / counts
    seq_ratio = jnp.sum(group_hot * group_ratio[None, :], 1)
    out_scale = jnp.pad(out_mask.astype(F32) / KEEP_OUTPUT, ((0, 0), (0, hid - hidden)))
    act_coef = 2.0 * ACTIVATION_COEF * seq_ratio[:, None] * out_scale * out_scale
    smooth_coef = jnp.broadcast_to(2.0 * TAR_BETA * seq_ratio[:, None], (seq_count, hid))
    length_wide = jnp.broadcast_to(lengths[:, None], (seq_count, hid))

    steps = block_steps(time_steps, 7)
    blocks = time_steps // steps

    def at_time(width, order=lambda b: b):
        return pl.BlockSpec((steps, seq_count, width), lambda b: (order(b), 0, 0))

    def fixed(*shape):
        return pl.BlockSpec(shape, lambda b: (0,) * len(shape))

    acts, cells, prev_low = pl.pallas_call(
        functools.partial(forward_kernel, hid),
        grid=(blocks,),
        in_specs=[at_time(wide), fixed(wide, 4 * hid), fixed(hid, 4 * hid)],
        out_specs=[at_time(4 * hid), at_time(hid), at_time(hid)],
        out_shape=[
            jax.ShapeDtypeStruct((time_steps, seq_count, 4 * hid), F32),
            jax.ShapeDtypeStruct((time_steps, seq_count, hid), F32),
            jax.ShapeDtypeStruct((time_steps, seq_count, hid), BF16),
        ],
        scratch_shapes=[
            pltpu.VMEM((steps * seq_count, 4 * hid), F32),
            pltpu.VMEM((seq_count, hid), F32),
            pltpu.VMEM((seq_count, hid), BF16),
        ],
        compiler_params=params(),
        name="forward",
    )(dropped, w_in_t, w_rec_t)

    def back(b):
        return blocks - 1 - b

    def before(b):
        return jnp.maximum(back(b) * steps - 1, 0)

    grads = pl.pallas_call(
        functools.partial(backward_kernel, hid),
        grid=(blocks,),
        in_specs=[
            at_time(4 * hid, back),
            at_time(hid, back),
            pl.BlockSpec((1, seq_count, hid), lambda b: (before(b), 0, 0)),
            pl.BlockSpec((1, seq_count, hid), lambda b: (before(b), 0, 3)),
            at_time(hid, back),
            fixed(seq_count, hid),
            fixed(seq_count, hid),
            fixed(seq_count, hid),
            fixed(seq_count, hid),
            fixed(4 * hid, hid),
        ],
        out_specs=at_time(4 * hid, back),
        out_shape=jax.ShapeDtypeStruct((time_steps, seq_count, 4 * hid), BF16),
        scratch_shapes=[pltpu.VMEM((seq_count, hid), F32)] * 3,
        compiler_params=params(),
        name="backward",
    )(
        acts,
        cells,
        cells,
        acts,
        cot_time,
        out_scale,
        act_coef,
        smooth_coef,
        length_wide,
        w_rec,
    )

    if row_count == hidden:
        own_rows = lax.dynamic_slice_in_dim(grads, row_at * hid, hid, 2)
    else:
        packed = grads.reshape(time_steps, seq_count, 4, hid)[..., :hidden]
        packed = packed.reshape(time_steps, seq_count, gates)
        own_rows = lax.dynamic_slice_in_dim(packed, row_at * row_count, row_count, 2)
        own_rows = jnp.pad(own_rows, ((0, 0), (0, 0), (0, -row_count % LANES)))
    own_wide = own_rows.shape[2]
    pick = jnp.broadcast_to((groups == 0).astype(BF16)[:, None], (seq_count, own_wide))
    part_in, part_rec = pl.pallas_call(
        weight_kernel,
        grid=(blocks,),
        in_specs=[
            at_time(own_wide),
            at_time(wide),
            at_time(hid),
            fixed(seq_count, own_wide),
        ],
        out_specs=[fixed(2, own_wide, wide), fixed(2, own_wide, hid)],
        out_shape=[
            jax.ShapeDtypeStruct((2, own_wide, wide), F32),
            jax.ShapeDtypeStruct((2, own_wide, hid), F32),
        ],
        compiler_params=params(),
        name="weights",
    )(own_rows, dropped, prev_low, pick)

    def split(block):
        total = jnp.concatenate(
            [block[0][:, : width_in + 1], block[1][:, :hidden] * w_scale], 1
        )
        return total

    def group_part(at):
        return split(
            (
                lax.dynamic_index_in_dim(part_in, at, 0, False)[:row_count],
                lax.dynamic_index_in_dim(part_rec, at, 0, False)[:row_count],
            )
        )

    other = flip(group_part(1 - grp_at).astype(BF16), "grp", 1)
    summed = group_part(grp_at) + other.astype(F32)
    columns = summed.shape[1]
    part_rows = ceil_to(row_count, seq_n) // seq_n
    summed = jnp.pad(summed, ((0, seq_n * part_rows - row_count), (0, 0)))
    sent = lax.all_to_all(
        summed.astype(BF16).reshape(seq_n, part_rows, columns), "seq", 0, 0, tiled=True
    )
    total = jnp.sum(sent.astype(F32), 0)
    total_low = total.astype(BF16)
    everyone = spread(total_low, "seq").reshape(seq_n * part_rows, columns)[:row_count]
    everyone = everyone.astype(F32)
    peer = flip(total_low, "grp", 1).astype(F32)
    self_dot = jnp.sum(total * total)
    cross_dot = jnp.sum(total * peer)
    mine_hot = (jnp.arange(2) == grp_at).astype(F32)
    local_gram = (
        mine_hot[:, None] * mine_hot[None, :] * self_dot
        + mine_hot[:, None] * (1.0 - mine_hot)[None, :] * cross_dot
    )
    gram = butterfly_sum(local_gram, ("grp", "seq", "row"))

    own_seqs = lax.dynamic_slice_in_dim(grads, row_at * share, share, 1)
    own_scale = lax.dynamic_slice_in_dim(in_scale, row_at * share, share, 0)
    input_time = jnp.einsum(
        "tsr,rk->tsk", own_seqs, w_in[:, :width_in], preferred_element_type=F32
    )
    input_grad = jnp.swapaxes(input_time * own_scale[None], 0, 1)
    return (
        input_grad,
        everyone[None, :, :width_in],
        everyone[None, :, width_in + 1 :],
        everyone[None, :, width_in],
        gram,
    )


def solution(mesh):
    return jax.shard_map(
        local,
        mesh=mesh,
        in_specs=(
            P(("grp", "seq"), None, None),
            P(("grp", "seq"), None),
            P(("grp", "seq"), None),
            P(("grp", "seq")),
            P(("grp", "seq")),
            P("row", None),
            P("row", None),
            P("row", None),
            P("row"),
            P(("grp", "seq"), None, None),
        ),
        out_specs=(
            P(("grp", "seq", "row"), None, None),
            P("grp", "row", None),
            P("grp", "row", None),
            P("grp", "row"),
            P(),
        ),
        check_vma=False,
    )
```

time: 4720 us -> 313 us (0.07)
  waiting for transfers between devices: 2650 us -> 55.5 us
  blocking collectives: 1150 us -> 7.98 us
  local copies, waits for them, and re-layouts: 459 us -> 57.7 us
  other arithmetic: 285 us -> 21.8 us
  matrix products: 144 us -> 10.8 us
  Pallas kernels: 0 us -> 131 us
    psum x71 -> x0, waiting for transfers between devices: 2400 us -> none  [the longest x70 2350 us: recur_back(): return lax.psum(partial_back, 'row')]
    all_gather x70 -> x0, blocking collectives: 1100 us -> none  [full_gates(): return lax.all_gather(partial_gates, 'row', axis=1, tiled=True)]
    reduce_scatter x3 -> x0, waiting for transfers between devices: 243 us -> none  [the longest x1 232 us: local(): lax.psum_scatter(jnp.einsum('slr,rk->slk', grad_seq, input_gate_weight, p...]
    another operation x145 -> x1, other arithmetic: 160 us -> 0.3 us
    dynamic_update_slice x210 -> x0, local copies, waits for them, and re-layouts: 153 us -> none  [the longest x140 102 us: local(): lax.scan(forward_step, start_state, projected)]
    dot_general x146 -> x1, matrix products: 144 us -> 10.8 us  [local(): jnp.einsum('tsr,rk->tsk', own_seqs, w_in[:, :width_in], preferred_element...]
    pallas_call x0 -> x3, Pallas kernels: none -> 131 us  [the longest x1 61.9 us: local(): pl.pallas_call(functools.partial(forward_kernel, hid), grid=(blocks,), in...]
    dynamic_slice x71 -> x3, local copies, waits for them, and re-layouts: 94.4 us -> 5.01 us  [the longest x1 4.94 us: local(): own_rows = lax.dynamic_slice_in_dim(grads, row_at * hid, hid, 2)]
  transfers between devices with their start and end apart: 75 -> 14, of which waited for: 74 -> 10; matrix products, arithmetic and copies ran while one was open for 3% -> 16% of each run, Pallas kernels for 0% -> 0%
where the time goes in v1:
time: 313 us; the launch traced here: 312 us
  Pallas kernels  131 us (42%)
  local copies, waits for them, and re-layouts  57.7 us (18%)
  waiting for transfers between devices  55.5 us (18%)
  starting transfers between devices  25.9 us (8%)
  other arithmetic  21.8 us (7%)
  matrix products  10.8 us (3%)
  blocking collectives  7.98 us (3%)
    pallas_call x1, Pallas kernels, local(): pl.pallas_call(functools.partial(forward_kernel, hid), grid=(blocks,), in...  61.9 us
    pallas_call x1, Pallas kernels, local(): pl.pallas_call(functools.partial(backward_kernel, hid), grid=(blocks,), i...  43.1 us
    pallas_call x1, Pallas kernels, local(): pl.pallas_call(weight_kernel, grid=(blocks,), in_specs=[at_time(own_wide)...  26.1 us
    all_to_all x3, waiting for transfers between devices, spread(): return lax.all_to_all(copies, axis, 0, 0, tiled=True)  19 us
    ppermute x10, waiting for transfers between devices, flip(): return lax.ppermute(block, axis, [(at, at ^ bit) for at in range(count)])  18.8 us
    all_to_all x1, waiting for transfers between devices, local(): lax.all_to_all(summed.astype(BF16).reshape(seq_n, part_rows, columns), 's...  17.8 us
    all_to_all x3, starting transfers between devices, spread(): return lax.all_to_all(copies, axis, 0, 0, tiled=True)  14.4 us
    dot_general x1, matrix products, local(): jnp.einsum('tsr,rk->tsk', own_seqs, w_in[:, :width_in], preferred_element...  10.8 us
  transfers between devices with their start and end apart: 14, of which 10 were waited for; matrix products, arithmetic and copies ran while one was open for 16% of the time, Pallas kernels for 0%

profile of v1, /device:TPU:0, one launch (start us, length us, event | category | flops | bytes accessed | tf_op | source)
XLA Modules:
  0.0 311.8 jit_solution(11619311898694020488)
XLA Ops:
  0.6 0.8 subtract_convert_fusion
  1.6 1.4 multiply_convert_fusion.1
  3.1 2.5 concatenate.14
  5.6 0.9 broadcast_in_dim.24
  6.6 6.3 %all-to-all-start = ((bf16[4,50,1552]{2,1,0:T(8,128)(2,1)}), bf16[4,50,1552]{2,1,0:T(8,128)(2,1)S(1)}, u32[]{:S(2)}, u32[]{:S(2)}) async-start(bf16[4,50,1552]{2,1,0:T(8,128)(2,1)} %broadcast_in_dim.24), calls=%async_computation | async-start | bytes 1490944 | tf_op jit(solution)/shard_map/all_to_all | solution.py:46
  13.1 19.0 %all-to-all-done = bf16[4,50,1552]{2,1,0:T(8,128)(2,1)S(1)} async-done(((bf16[4,50,1552]{2,1,0:T(8,128)(2,1)}), bf16[4,50,1552]{2,1,0:T(8,128)(2,1)S(1)}, u32[]{:S(2)}, u32[]{:S(2)}) %all-to-all-start) | async-done | bytes 620832 | tf_op jit(solution)/shard_map/all_to_all | solution.py:46
  32.4 2.2 broadcast_in_dim.25
  34.6 3.7 %all-to-all-start.1 = ((bf16[4,4,50,1552]{3,1,2,0:T(4,128)(2,1)}), bf16[4,4,50,1552]{3,1,2,0:T(4,128)(2,1)S(1)}, u32[]{:S(2)}, u32[]{:S(2)}) async-start(bf16[4,4,50,1552]{3,1,2,0:T(4,128)(2,1)} %broadcast_in_dim.25), calls=%async_computation.1 | async-start | bytes 5324800 | tf_op jit(solution)/shard_map/all_to_all | solution.py:46
  38.3 10.6 %fusion = bf16[70,64,1150]{2,1,0:T(8,128)(2,1)} fusion(bf16[64,70,1150]{2,0,1:T(8,128)(2,1)} %param.10, f32[64,1150]{1,0:T(8,128)S(1)} %convert_multiply_fusion.1), kind=kLoop, calls=%fused_computation.1 | loop fusion | flops 15456000 | bytes 20902400 | tf_op jit(solution)/shard_map/convert_element_type | solution.py:238
  48.9 5.4 %pad.19.cot_ref = bf16[70,64,512]{2,1,0:T(8,128)(2,1)} pad(bf16[70,64,400]{2,1,0:T(8,128)(2,1)} %bitcast.38, bf16[]{:T(256)} %constant.59.clone.1), padding=0_0x0_0x0_112 | pad | bytes 8171522 | tf_op jit(solution)/shard_map/jit(_pad)/pad | solution.py:247
  54.3 9.3 %concatenate.13.drop_ref = bf16[70,64,1152]{2,1,0:T(8,128)(2,1)} pad(bf16[70,64,1150]{2,1,0:T(8,128)(2,1)} %fusion, bf16[]{:T(256)} %constant.21.clone.1), padding=0_0x0_0x0_2 | pad | bytes 20625922 | tf_op jit(solution)/shard_map/concatenate | solution.py:239
  63.6 2.1 collective-permute-start.1
  65.7 3.0 collective-permute-done.1
  68.7 1.5 collective-permute-start.2
  70.2 2.1 collective-permute-done.2
  72.2 0.6 fusion.6
  72.8 0.6 broadcast_divide_fusion
  73.6 0.7 multiply_multiply_fusion
  74.3 1.4 broadcast_in_dim.26
  75.7 8.0 %all_to_all.25 = bf16[2,4,4,50,1552]{4,2,3,1,0:T(4,128)(2,1)S(1)} all-to-all(bf16[2,4,4,50,1552]{4,2,3,1,0:T(4,128)(2,1)S(1)} %broadcast_in_dim.26), channel_id=1, replica_groups=mesh['grp'=2,'seq'=4,'row'=4] {'grp'}, dimensions={0} | all-to-all | bytes 9932800 | tf_op jit(solution)/shard_map/all_to_all | solution.py:46
  83.7 0.6 copy.34
  84.3 0.5 pad.17.clone
  85.0 2.9 slice_bitcast_fusion.2
  87.9 1.3 copy-done
  89.2 1.7 fusion.7
  90.9 2.5 copy.33.wrec_ref
  93.3 6.7 %copy.32.win_ref = bf16[1152,2048]{1,0:T(8,128)(2,1)} copy(bf16[1152,2048]{0,1:T(8,128)(2,1)} %slice_bitcast_fusion.2) | data formatting | bytes 9437184 | tf_op jit(solution)/shard_map/transpose | solution.py:233
  100.1 61.9 %forward.1 = (f32[70,64,2048]{2,1,0:T(8,128)}, f32[70,64,512]{2,1,0:T(8,128)}, bf16[70,64,512]{2,1,0:T(8,128)(2,1)}) custom-call(bf16[70,64,1152]{2,1,0:T(8,128)(2,1)} %concatenate.13.drop_ref, bf16[1152,2048]{1,0:T(8,128)(2,1)} %copy.32.win_ref, bf16[512,2048]{1,0:T(8,128)(2,1)} %copy.33.wrec_ref), custom_call_target="tpu_custom_call" | custom-call | tf_op jit(solution)/shard_map/forward/pallas_call | solution.py:269
  162.0 0.7 broadcast_in_dim.27.smooth_ref
  162.7 0.7 broadcast_in_dim.28.length_ref
  163.4 43.1 %backward.1 = bf16[70,64,2048]{2,1,0:T(8,128)(2,1)} custom-call(f32[70,64,2048]{2,1,0:T(8,128)} %get-tuple-element.10.act_ref.out_before_ref, f32[70,64,512]{2,1,0:T(8,128)} %get-tuple-element.11.cell_ref.before_ref, f32[70,64,512]{2,1,0:T(8,128)} %get-tuple-element.11.cell_ref.before_ref, f32[70,64,2048]{2,1,0:T(8,128)} %get-tuple-element.10.act_ref.out_before_ref, ...), custom_call_target="tpu_custom_call" | custom-call | tf_op jit(solution)/shard_map/backward/pallas_call | solution.py:294
  206.5 4.9 %constant_dynamic-slice_fusion.rows_ref = bf16[70,64,512]{2,1,0:T(8,128)(2,1)} fusion(bf16[70,64,2048]{2,1,0:T(8,128)(2,1)} %backward.1, s32[]{:T(128)S(6)} %select_n.22), kind=kLoop, calls=%fused_computation.28 | loop fusion | bytes 9175044 | tf_op jit(solution)/shard_map/dynamic_slice | solution.py:328
  211.5 0.7 broadcast_in_dim.29.pick_ref
  212.2 26.1 %weights.1 = (f32[2,512,1152]{2,1,0:T(8,128)}, f32[2,512,512]{2,1,0:T(8,128)}) custom-call(bf16[70,64,512]{2,1,0:T(8,128)(2,1)} %constant_dynamic-slice_fusion.rows_ref, bf16[70,64,1152]{2,1,0:T(8,128)(2,1)} %concatenate.13.drop_ref, bf16[70,64,512]{2,1,0:T(8,128)(2,1)} %get-tuple-element.12.prev_ref, bf16[64,512]{1,0:T(8,128)(2,1)} %broadcast_in_dim.29.pick_ref), custom_call_target="tpu_custom_call" | custom-call | tf_op jit(solution)/shard_map/weights/pallas_call | solution.py:336
  238.2 1.7 fusion.3
  239.9 1.5 dynamic-slice_bitcast_fusion.1
  241.5 0.3 fusion.4
  242.0 0.3 collective-permute-start.3
  242.3 1.6 dynamic-slice_bitcast_fusion
  243.9 1.2 collective-permute-done.3
  245.2 0.5 fusion.2
  245.7 1.2 reshape.67
  246.9 3.5 %all-to-all-start.3 = ((bf16[4,100,1551]{2,1,0:T(8,128)(2,1)}), bf16[4,100,1551]{2,1,0:T(8,128)(2,1)S(1)}, u32[]{:S(2)}, u32[]{:S(2)}) async-start(bf16[4,100,1551]{2,1,0:T(8,128)(2,1)} %reshape.67), calls=%async_computation.3 | async-start | bytes 2768896 | tf_op jit(solution)/shard_map/all_to_all | solution.py:373
  250.5 17.8 %all-to-all-done.3 = bf16[4,100,1551]{2,1,0:T(8,128)(2,1)S(1)} async-done(((bf16[4,100,1551]{2,1,0:T(8,128)(2,1)}), bf16[4,100,1551]{2,1,0:T(8,128)(2,1)S(1)}, u32[]{:S(2)}, u32[]{:S(2)}) %all-to-all-start.3) | async-done | bytes 1240832 | tf_op jit(solution)/shard_map/all_to_all | solution.py:373
  268.6 1.2 broadcast_in_dim.30
  269.8 4.3 %all-to-all-start.4 = ((bf16[4,100,1551]{2,1,0:T(8,128)(2,1)}), bf16[4,100,1551]{2,1,0:T(8,128)(2,1)}, u32[]{:S(2)}, u32[]{:S(2)}) async-start(bf16[4,100,1551]{2,1,0:T(8,128)(2,1)} %broadcast_in_dim.30), calls=%async_computation.4 | async-start | bytes 2768896 | tf_op jit(solution)/shard_map/all_to_all | solution.py:46
  274.1 10.8 %multiply_bitcast_fusion = f32[16,70,1150]{2,0,1:T(8,128)} fusion(bf16[2048,1552]{1,0:T(8,128)(2,1)} %bitcast.35, bf16[70,64,2048]{2,1,0:T(8,128)(2,1)} %backward.1, s32[]{:T(128)S(6)} %select_n.21, f32[16,1150]{1,0:T(8,128)S(1)} %constant_dynamic-slice_fusion.1), kind=kOutput, calls=%fused_computation.2 | convolution fusion | flops 5276936192 | bytes 14531716 | tf_op jit(solution)/shard_map/tsr,rk->tsk/dot_general | solution.py:392
  285.0 0.8 multiply_reduce_fusion.1
  285.8 1.4 multiply_add_fusion
  287.1 0.5 collective-permute-start.5
  287.6 0.8 collective-permute-done.5
  288.5 1.4 fusion.8
  289.8 1.8 collective-permute-start.6
  291.6 1.8 collective-permute-done.6
  293.4 1.4 fusion.9
  294.8 1.8 collective-permute-start.7
  296.5 1.8 collective-permute-done.7
  298.3 3.6 %collective-permute-done.8 = f32[2,2]{1,0:T(2,128)S(1)} collective-permute-done((f32[2,2]{1,0:T(2,128)S(1)}, f32[2,2]{1,0:T(2,128)S(1)}, u32[]{:S(2)}, u32[]{:S(2)}) %collective-permute-start.8) | collective-permute-done | bytes 48 | tf_op jit(solution)/shard_map/ppermute | solution.py:27
  301.9 4.5 %collective-permute-done.9 = f32[2,2]{1,0:T(2,128)S(1)} collective-permute-done((f32[2,2]{1,0:T(2,128)S(1)}, f32[2,2]{1,0:T(2,128)S(1)}, u32[]{:S(2)}, u32[]{:S(2)}) %collective-permute-start.9) | collective-permute-done | bytes 48 | tf_op jit(solution)/shard_map/ppermute | solution.py:27
  306.4 0.6 add.79
  306.9 1.5 reshape.68
  308.5 0.8 slice_reduce_fusion
  309.3 1.2 slice_bitcast_fusion.4
  310.5 1.4 slice_bitcast_fusion.3
  (41 shorter events, 1.7 us)
Async XLA Ops:
  3.1 9.8 %copy-start.4 = (s32[64]{0:T(128)S(1)}, s32[64]{0:T(128)}, u32[]{:S(2)}) copy-start(s32[64]{0:T(128)} %param.13) | copy-start | bytes 772
  3.1 9.8 %copy-start.5 = (s32[64]{0:T(128)S(1)}, s32[64]{0:T(128)}, u32[]{:S(2)}) copy-start(s32[64]{0:T(128)} %param.14) | copy-start | bytes 772
  3.1 10.0 %copy-start.2 = (s32[64,1150]{1,0:T(8,128)S(1)}, s32[64,1150]{1,0:T(8,128)}, u32[]{:S(2)}) copy-start(s32[64,1150]{1,0:T(8,128)} %param.11) | copy-start | bytes 883204
  6.6 25.5 %all-to-all-start = ((bf16[4,50,1552]{2,1,0:T(8,128)(2,1)}), bf16[4,50,1552]{2,1,0:T(8,128)(2,1)S(1)}, u32[]{:S(2)}, u32[]{:S(2)}) async-start(bf16[4,50,1552]{2,1,0:T(8,128)(2,1)} %broadcast_in_dim.24), calls=%async_computation | async-start | bytes 1490944 | tf_op jit(solution)/shard_map/all_to_all | solution.py:46
  13.0 50.6 %collective-permute-start = (f32[2]{0:T(128)S(1)}, f32[2]{0:T(128)S(1)}, u32[]{:S(2)}, u32[]{:S(2)}) collective-permute-start(f32[2]{0:T(128)S(1)} %select_reduce_fusion.1), channel_id=1, source_target_pairs={{0,16},{16,0},{1,17},{17,1},{2,18},{18,2},{3,19},{19,3},{4,20},{20... | collective-permute-start | bytes 32 | tf_op jit(solution)/shard_map/ppermute | solution.py:27
  34.6 39.8 %all-to-all-start.1 = ((bf16[4,4,50,1552]{3,1,2,0:T(4,128)(2,1)}), bf16[4,4,50,1552]{3,1,2,0:T(4,128)(2,1)S(1)}, u32[]{:S(2)}, u32[]{:S(2)}) async-start(bf16[4,4,50,1552]{3,1,2,0:T(4,128)(2,1)} %broadcast_in_dim.25), calls=%async_computation.1 | async-start | bytes 5324800 | tf_op jit(solution)/shard_map/all_to_all | solution.py:46
  54.3 9.3 %copy-start.3 = (s32[64,400]{1,0:T(8,128)S(1)}, s32[64,400]{1,0:T(8,128)}, u32[]{:S(2)}) copy-start(s32[64,400]{1,0:T(8,128)} %param.12) | copy-start | bytes 307204
  63.6 5.1 %collective-permute-start.1 = (f32[2]{0:T(128)S(1)}, f32[2]{0:T(128)S(1)}, u32[]{:S(2)}, u32[]{:S(2)}) collective-permute-start(f32[2]{0:T(128)S(1)} %add.66), channel_id=1, source_target_pairs={{0,4},{4,0},{8,12},{12,8},{1,5},{5,1},{9,13},{13,9},{2,6},{6,2},{1... | collective-permute-start | bytes 32 | tf_op jit(solution)/shard_map/ppermute | solution.py:27
  68.7 3.5 %collective-permute-start.2 = (f32[2]{0:T(128)S(1)}, f32[2]{0:T(128)S(1)}, u32[]{:S(2)}, u32[]{:S(2)}) collective-permute-start(f32[2]{0:T(128)S(1)} %add.67), channel_id=1, source_target_pairs={{0,8},{4,12},{8,0},{12,4},{1,9},{5,13},{9,1},{13,5},{2,10},{6,14},... | collective-permute-start | bytes 32 | tf_op jit(solution)/shard_map/ppermute | solution.py:27
  84.8 4.3 %copy-start = (bf16[4,512,1552]{2,1,0:T(8,128)(2,1)}, bf16[4,512,1552]{2,1,0:T(8,128)(2,1)S(1)}, u32[]{:S(2)}) copy-start(bf16[4,512,1552]{2,1,0:T(8,128)(2,1)S(1)} %pad.17.clone) | copy-start | bytes 19070980
  238.2 3.2 %copy-start.1 = (s32[400,400]{1,0:T(8,128)S(1)}, s32[400,400]{1,0:T(8,128)}, u32[]{:S(2)}) copy-start(s32[400,400]{1,0:T(8,128)} %param.17) | copy-start | bytes 1920004
  242.0 3.1 %collective-permute-start.3 = (bf16[400,1551]{1,0:T(8,128)(2,1)S(1)}, bf16[400,1551]{1,0:T(8,128)(2,1)S(1)}, u32[]{:S(2)}, u32[]{:S(2)}) collective-permute-start(bf16[400,1551]{1,0:T(8,128)(2,1)S(1)} %pad_maximum_fusion), channel_id=1, source_target_pairs={{0,16},{16,0},{1,17},{17,1},{2,18},{18,2},{3,19},{19,3},{4,20},{20... | collective-permute-start | bytes 3722408 | tf_op jit(solution)/shard_map/ppermute | solution.py:27
  246.9 21.4 %all-to-all-start.3 = ((bf16[4,100,1551]{2,1,0:T(8,128)(2,1)}), bf16[4,100,1551]{2,1,0:T(8,128)(2,1)S(1)}, u32[]{:S(2)}, u32[]{:S(2)}) async-start(bf16[4,100,1551]{2,1,0:T(8,128)(2,1)} %reshape.67), calls=%async_computation.3 | async-start | bytes 2768896 | tf_op jit(solution)/shard_map/all_to_all | solution.py:373
  268.5 16.4 %collective-permute-start.4 = (bf16[100,1551]{1,0:T(8,128)(2,1)S(1)}, bf16[100,1551]{1,0:T(8,128)(2,1)S(1)}, u32[]{:S(2)}, u32[]{:S(2)}) collective-permute-start(bf16[100,1551]{1,0:T(8,128)(2,1)S(1)} %convert_element_type.105), channel_id=1, source_target_pairs={{0,16},{16,0},{1,17},{17,1},{2,18},{18,2},{3,19},{19,3},{4,20},{20... | collective-permute-start | bytes 930608 | tf_op jit(solution)/shard_map/ppermute | solution.py:27
  269.8 37.1 %all-to-all-start.4 = ((bf16[4,100,1551]{2,1,0:T(8,128)(2,1)}), bf16[4,100,1551]{2,1,0:T(8,128)(2,1)}, u32[]{:S(2)}, u32[]{:S(2)}) async-start(bf16[4,100,1551]{2,1,0:T(8,128)(2,1)} %broadcast_in_dim.30), calls=%async_computation.4 | async-start | bytes 2768896 | tf_op jit(solution)/shard_map/all_to_all | solution.py:46
  287.1 1.3 collective-permute-start.5
  289.8 3.6 %collective-permute-start.6 = (f32[2,2]{1,0:T(2,128)S(1)}, f32[2,2]{1,0:T(2,128)S(1)}, u32[]{:S(2)}, u32[]{:S(2)}) collective-permute-start(f32[2,2]{1,0:T(2,128)S(1)} %fusion.8), channel_id=1, source_target_pairs={{0,4},{4,0},{8,12},{12,8},{1,5},{5,1},{9,13},{13,9},{2,6},{6,2},{1... | collective-permute-start | bytes 56 | tf_op jit(solution)/shard_map/ppermute | solution.py:27
  294.8 3.6 %collective-permute-start.7 = (f32[2,2]{1,0:T(2,128)S(1)}, f32[2,2]{1,0:T(2,128)S(1)}, u32[]{:S(2)}, u32[]{:S(2)}) collective-permute-start(f32[2,2]{1,0:T(2,128)S(1)} %fusion.9), channel_id=1, source_target_pairs={{0,8},{4,12},{8,0},{12,4},{1,9},{5,13},{9,1},{13,5},{2,10},{6,14},... | collective-permute-start | bytes 56 | tf_op jit(solution)/shard_map/ppermute | solution.py:27
  298.3 3.6 %collective-permute-start.8 = (f32[2,2]{1,0:T(2,128)S(1)}, f32[2,2]{1,0:T(2,128)S(1)}, u32[]{:S(2)}, u32[]{:S(2)}) collective-permute-start(f32[2,2]{1,0:T(2,128)S(1)} %add.77), channel_id=1, source_target_pairs={{0,1},{1,0},{2,3},{3,2},{4,5},{5,4},{6,7},{7,6},{8,9},{9,8},{10,11... | collective-permute-start | bytes 56 | tf_op jit(solution)/shard_map/ppermute | solution.py:27
  301.9 4.5 %collective-permute-start.9 = (f32[2,2]{1,0:T(2,128)S(1)}, f32[2,2]{1,0:T(2,128)S(1)}, u32[]{:S(2)}, u32[]{:S(2)}) collective-permute-start(f32[2,2]{1,0:T(2,128)S(1)} %add.78), channel_id=1, source_target_pairs={{0,2},{1,3},{2,0},{3,1},{4,6},{5,7},{6,4},{7,5},{8,10},{9,11},{10,... | collective-permute-start | bytes 56 | tf_op jit(solution)/shard_map/ppermute | solution.py:27
